TPU v7x, 256 devices: a whole 4x4x8 slice. The times are simulated.
256 devices in a mesh: ctx: 64 (over y_hi, z, x), tp: 4 (over y_lo, core).
Axes of the slice: x: 4, y: 4 (y_hi: 2, y_lo: 2; y = y_hi * 2 + y_lo), z: 8, core: 2. Of those that a mesh axis runs over, the one named last changes fastest.
Arguments:
- ids: int32 [32768], P('ctx'), may hold values from 0 to 511
- embed_table: bfloat16 [512, 4096], P(None, 'tp'), may hold values from -126 to 126
- norm_gain: float32 [4096], replicated, may hold values from 0.1 to 1.9
- in_weight: bfloat16 [3, 4096, 4096], P(None, 'ctx', 'tp'), may hold values from -0.09375 to 0.09375
- in_scale: float32 [3, 4096], P(None, 'tp'), may hold values from 0.1 to 1.9
- short_filter: float32 [3, 7, 4096], P(None, None, 'tp'), may hold values from -2.4 to 2.4
- long_filter: float32 [128, 256], P(None, 'tp'), may hold values from -0.9 to 0.9
- decay: float32 [256], P('tp'), may hold values from 0.003 to 0.1
Outputs:
- mixed: bfloat16 [32768, 4096], P('ctx', 'tp')
All inputs are finite; a program needn't handle non-finite values.
Results may differ from a plain program's by a relative error of at most 0.009.
Values may be sent and summed in bfloat16 or wider, within the bound.
No kernel may reach another device: no remote copies, remote signals or barrier semaphores. Data moves between devices by JAX's collectives and lax.ppermute only.
A program may use at most 128 MiB of HBM per device.

v0:
```python
import jax
import jax.numpy as jnp
from jax import lax
from jax.sharding import PartitionSpec as P

GROUP = 16
SHORT_TAPS = 7
LONG_TAPS = 128


def passed_along(value, axis, steps):
    count = lax.axis_size(axis)
    pairs = [(source, (source + steps) % count) for source in range(count)]
    return lax.ppermute(value, axis, pairs)


def toeplitz(long_filter, decay):
    steps = jnp.arange(LONG_TAPS, dtype=jnp.float32)
    taps = (long_filter * jnp.exp(-decay[None, :] * steps[:, None])).astype(jnp.bfloat16)
    offset = (
        jnp.arange(LONG_TAPS, dtype=jnp.int32)[:, None]
        - jnp.arange(LONG_TAPS, dtype=jnp.int32)[None, :]
    )
    lower = jnp.take(taps, jnp.clip(offset, 0, LONG_TAPS - 1), axis=0)
    upper = jnp.take(taps, jnp.clip(offset + LONG_TAPS, 0, LONG_TAPS - 1), axis=0)
    zero_tap = jnp.zeros((), jnp.bfloat16)
    toep_near = jnp.where((offset >= 0)[:, :, None], lower, zero_tap)
    toep_far = jnp.where((offset < 0)[:, :, None], upper, zero_tap)
    return (toep_near, toep_far)


def short_conv(extended, filt, out_len):
    margin = SHORT_TAPS - 1
    total = jnp.zeros((extended.shape[0], out_len, extended.shape[2]), jnp.float32)
    for k in range(SHORT_TAPS):
        window = extended[:, margin - k : margin - k + out_len, :].astype(jnp.float32)
        total = total + filt[:, k, None, :] * window
    return total


def per_device(ids, embed_table, norm_gain, in_weight, in_scale, short_filter, long_filter, decay):
    rows = ids.shape[0]
    vocab = embed_table.shape[0]
    width_local = embed_table.shape[1]
    onehot = (ids[:, None] == lax.iota(jnp.int32, vocab)[None, :]).astype(jnp.bfloat16)
    local = jnp.dot(onehot, embed_table, preferred_element_type=jnp.float32).astype(jnp.bfloat16)
    local_f = local.astype(jnp.float32)
    total = lax.psum(jnp.sum(local_f * local_f, axis=1), "tp")
    full_width = width_local * lax.axis_size("tp")
    gain = lax.dynamic_slice_in_dim(norm_gain, lax.axis_index("tp") * width_local, width_local, 0)
    scaled = local_f * lax.rsqrt(total[:, None] / full_width + 1e-06) * gain[None, :]
    features = lax.all_gather(scaled.astype(jnp.bfloat16), "tp", axis=1, tiled=True)

    def add_one(piece):
        return jnp.dot(features, piece, preferred_element_type=jnp.float32)

    def project_stream(weight):
        return add_one(lax.all_gather(weight, "ctx", axis=0, tiled=True))

    summed = jnp.stack([project_stream(in_weight[p]) for p in range(3)], axis=0)
    proj = (summed * in_scale[:, None, :]).astype(jnp.bfloat16)
    margin = SHORT_TAPS - 1
    before = passed_along(proj[:, rows - margin :, :], "ctx", 1)
    streams = short_conv(jnp.concatenate([before, proj], axis=1), short_filter, rows)
    gate = streams[0]
    inner = (streams[1] * streams[2]).astype(jnp.bfloat16)
    previous = passed_along(inner[rows - LONG_TAPS :], "ctx", 1)
    extended = jnp.concatenate([previous, inner], axis=0)
    groups_local = long_filter.shape[1]
    blocks = extended.reshape(rows // LONG_TAPS + 1, LONG_TAPS, groups_local, GROUP)
    toep_near, toep_far = toeplitz(long_filter, decay)
    conv = jnp.einsum("tsg,bsgc->btgc", toep_near, blocks[1:], preferred_element_type=jnp.float32)
    conv = conv + jnp.einsum(
        "tsg,bsgc->btgc", toep_far, blocks[:-1], preferred_element_type=jnp.float32
    )
    conv = conv.reshape(rows, width_local)
    return (gate * conv).astype(jnp.bfloat16)


def solution(mesh):
    placed = (
        P("ctx"),
        P(None, "tp"),
        P(),
        P(None, "ctx", "tp"),
        P(None, "tp"),
        P(None, None, "tp"),
        P(None, "tp"),
        P("tp"),
    )
    return jax.shard_map(
        per_device, mesh=mesh, in_specs=placed, out_specs=P("ctx", "tp"), check_vma=False
    )
```

profile of v0, /device:TPU:8, one launch (start us, length us, event | category | flops | bytes accessed | tf_op | source)
XLA Modules:
  0.0 709.9 jit_solution(41815037206658026)
XLA Ops:
  9.3 5.7 psum.7
  19.6 48.7 %all-gather.8.cloned.1.call-done = bf16[512,4096]{1,0:T(8,128)(2,1)} async-done(((bf16[512,1024]{1,0:T(8,128)(2,1)}), bf16[512,4096]{1,0:T(8,128)(2,1)}) %all-gather.8.cloned.1.call-update) | async-done | bytes 4194320 | tf_op jit(solution)/shard_map/all_gather | solution.py:52
  68.4 152.4 %all-gather.10.cloned.1.call-done = bf16[1,4096,1024]{2,1,0:T(8,128)(2,1)} async-done(((bf16[1,64,1024]{2,1,0:T(8,128)(2,1)}), bf16[1,4096,1024]{2,1,0:T(8,128)(2,1)}) %all-gather.10.cloned.1.call-update) | async-done | bytes 8388624 | tf_op jit(solution)/shard_map/all_gather | solution.py:58
  220.8 8.1 %fusion.26 = f32[1,512,1024]{2,1,0:T(8,128)S(1)} fusion(bf16[512,4096]{1,0:T(8,128)(2,1)} %all-gather.8.cloned.1.call-done, bf16[1,4096,1024]{2,1,0:T(8,128)(2,1)} %all-gather.10.cloned.1.call-done), kind=kOutput, calls=%fused_computation.47 | convolution fusion | flops 4294967296 | bytes 14680064 | tf_op jit(solution)/shard_map/dot_general | solution.py:55
  228.9 139.4 %all-gather.12.cloned.1.call-done = bf16[1,4096,1024]{2,1,0:T(8,128)(2,1)} async-done(((bf16[1,64,1024]{2,1,0:T(8,128)(2,1)}), bf16[1,4096,1024]{2,1,0:T(8,128)(2,1)}) %all-gather.12.cloned.1.call-update) | async-done | bytes 8388624 | tf_op jit(solution)/shard_map/all_gather | solution.py:58
  368.3 10.5 %fusion.29 = f32[1,512,1024]{2,1,0:T(8,128)} fusion(bf16[512,4096]{1,0:T(8,128)(2,1)} %all-gather.8.cloned.1.call-done, bf16[1,4096,1024]{2,1,0:T(8,128)(2,1)} %all-gather.12.cloned.1.call-done), kind=kOutput, calls=%fused_computation.48 | convolution fusion | flops 4294967296 | bytes 14680064 | tf_op jit(solution)/shard_map/dot_general | solution.py:55
  378.7 136.9 %all-gather.14.cloned.1.call-done = bf16[1,4096,1024]{2,1,0:T(8,128)(2,1)} async-done(((bf16[1,64,1024]{2,1,0:T(8,128)(2,1)}), bf16[1,4096,1024]{2,1,0:T(8,128)(2,1)}) %all-gather.14.cloned.1.call-update) | async-done | bytes 8388624 | tf_op jit(solution)/shard_map/all_gather | solution.py:58
  515.6 8.3 %fusion.32 = f32[1,512,1024]{2,1,0:T(8,128)S(1)} fusion(bf16[512,4096]{1,0:T(8,128)(2,1)} %all-gather.8.cloned.1.call-done, bf16[1,4096,1024]{2,1,0:T(8,128)(2,1)} %all-gather.14.cloned.1.call-done), kind=kOutput, calls=%fused_computation.49 | convolution fusion | flops 4294967296 | bytes 14680064 | tf_op jit(solution)/shard_map/dot_general | solution.py:55
  524.9 1.7 copy-done.3
  526.6 1.7 collective-permute-start
  528.3 57.8 %gather_fusion.1 = bf16[16384,64]{1,0:T(8,128)(2,1)} fusion(bf16[128,64]{1,0:T(8,128)(2,1)S(1)} %multiply_convert_fusion, s32[16384]{0:T(1024)S(1)} %bitcast_clamp_fusion), kind=kCustom, calls=%fused_computation.1.clone | custom fusion | bytes 4259840 | tf_op jit(solution)/shard_map/jit(_take)/gather | solution.py:25
  586.2 5.7 copy.20
  591.9 57.8 %gather_fusion = bf16[16384,64]{1,0:T(8,128)(2,1)} fusion(bf16[128,64]{1,0:T(8,128)(2,1)S(1)} %multiply_convert_fusion, s32[16384]{0:T(1024)S(1)} %bitcast_clamp_fusion.1), kind=kCustom, calls=%fused_computation.clone | custom fusion | bytes 4259840 | tf_op jit(solution)/shard_map/jit(_take)/gather | solution.py:24
  649.7 4.8 copy.17
  654.5 13.6 %multiply_add_fusion = f32[3,512,1024]{2,1,0:T(8,128)S(1)} fusion(bf16[3,512,1024]{2,1,0:T(8,128)(2,1)} %copy-done.3, bf16[3,6,1024]{2,1,0:T(8,128)(2,1)S(1)} %collective-permute-done, f32[3,1024]{1,0:T(4,128)S(1)} %get-tuple-element.18, f32[3,1024]{1,0:T(4,128)S(1)} %get-tuple-element.19, f32[3,1024]{1,0:T(4,128)S(1)} %get-tuple-element.20, ...), kind=kLoop, calls=%fused_computation.15 | loop fusion | flops 59768832 | bytes 9560064 | tf_op jit(solution)/shard_map/add | solution.py:37
  668.1 2.6 copy-done.2
  675.9 2.5 fusion.62
  678.5 6.9 collective-permute-done.1
  686.5 2.3 copy.19
  688.7 2.1 slice.97
  690.9 3.5 fusion.18
  694.3 1.6 add_bitcast_fusion
  698.5 2.0 copy.23
  700.5 2.9 fusion.17
  (54 shorter events, 17.0 us)
Async XLA Ops:
  6.5 1.2 copy-start
  6.5 10.5 %copy-start.5 = (bf16[3,64,1024]{2,1,0:T(8,128)(2,1)S(1)}, bf16[3,64,1024]{2,1,0:T(8,128)(2,1)}, u32[]{:S(2)}) copy-start(bf16[3,64,1024]{2,1,0:T(8,128)(2,1)} %param.13) | copy-start | bytes 1179652
  6.5 12.7 %copy-start.7 = (f32[128,64]{0,1:T(8,128)S(1)}, f32[128,64]{0,1:T(8,128)}, u32[]{:S(2)}) copy-start(f32[128,64]{0,1:T(8,128)} %param.16) | copy-start | bytes 98308
  6.5 12.8 %copy-start.9 = (f32[64]{0:T(128)S(1)}, f32[64]{0:T(128)}, u32[]{:S(2)}) copy-start(f32[64]{0:T(128)} %param.17) | copy-start | bytes 772
  6.5 12.9 %copy-start.6 = (f32[3,7,1024]{2,1,0:T(8,128)S(1)}, f32[3,7,1024]{2,1,0:T(8,128)}, u32[]{:S(2)}) copy-start(f32[3,7,1024]{2,1,0:T(8,128)} %param.15) | copy-start | bytes 258052
  6.5 61.8 %all-gather.8.cloned.1.call-start = ((), (), s32[]{:S(2)}) async-start(), calls=%async_computation | async-start | bytes 5242880 | tf_op jit(solution)/shard_map/all_gather | solution.py:52
  17.0 203.7 %all-gather.10.cloned.1.call-start = ((), (), s32[]{:S(2)}) async-start(), calls=%async_computation.1 | async-start | bytes 8519680 | tf_op jit(solution)/shard_map/all_gather | solution.py:58
  17.9 350.4 %all-gather.12.cloned.1.call-start = ((), (), s32[]{:S(2)}) async-start(), calls=%async_computation.2 | async-start | bytes 8519680 | tf_op jit(solution)/shard_map/all_gather | solution.py:58
  18.6 497.0 %all-gather.14.cloned.1.call-start = ((), (), s32[]{:S(2)}) async-start(), calls=%async_computation.3 | async-start | bytes 8519680 | tf_op jit(solution)/shard_map/all_gather | solution.py:58
  378.7 145.2 %copy-start.8 = (f32[3,1024]{1,0:T(4,128)S(1)}, f32[3,1024]{1,0:T(4,128)}, u32[]{:S(2)}) copy-start(f32[3,1024]{1,0:T(4,128)} %param.14) | copy-start | bytes 36868
  515.6 8.3 %copy-start.4 = (f32[1,512,1024]{2,1,0:T(8,128)S(1)}, f32[1,512,1024]{2,1,0:T(8,128)}, u32[]{:S(2)}) copy-start(f32[1,512,1024]{2,1,0:T(8,128)} %fusion.29) | copy-start | bytes 6291460
  524.9 1.7 copy-start.3
  526.6 128.0 %collective-permute-start = (bf16[3,6,1024]{2,1,0:T(8,128)(2,1)S(1)}, bf16[3,6,1024]{2,1,0:T(8,128)(2,1)S(1)}, u32[]{:S(2)}, u32[]{:S(2)}) collective-permute-start(bf16[3,6,1024]{2,1,0:T(8,128)(2,1)S(1)} %slice.102), channel_id=1, source_target_pairs={{0,4},{4,8},{8,12},{12,16},{16,20},{20,24},{24,28},{28,32},{32,36}... | collective-permute-start | bytes 110600 | tf_op jit(solution)/shard_map/ppermute | solution.py:14
  668.1 2.7 copy-start.2
  673.1 12.3 %collective-permute-start.1 = (bf16[128,1024]{1,0:T(8,128)(2,1)}, bf16[128,1024]{1,0:T(8,128)(2,1)S(1)}, u32[]{:S(2)}, u32[]{:S(2)}) collective-permute-start(bf16[128,1024]{1,0:T(8,128)(2,1)} %slice_bitcast_fusion.1), channel_id=1, source_target_pairs={{0,4},{4,8},{8,12},{12,16},{16,20},{20,24},{24,28},{28,32},{32,36}... | collective-permute-start | bytes 786440 | tf_op jit(solution)/shard_map/ppermute | solution.py:14
  698.5 4.9 copy-start.1
Sparse Core Ops, SparseCore 0:
  17.1 51.1 all-gather.7
  71.9 148.8 all-gather.9
  224.2 143.9 all-gather.11
  371.6 143.9 all-gather.13
where the time goes:
time: 710 us
  waiting for transfers between devices  486 us (68%)
  local copies, waits for them, and re-layouts  146 us (21%)
  matrix products  33.5 us (5%)
  other arithmetic  22.8 us (3%)
  between operations  13.4 us (2%)
    all_gather x3, waiting for transfers between devices, project_stream(): return add_one(lax.all_gather(weight, 'ctx', axis=0, tiled=True))  429 us
    gather x2, local copies, waits for them, and re-layouts, toeplitz(): jnp.take(taps, jnp.clip(offset + LONG_TAPS, 0, LONG_TAPS - 1), axis=0)  63.5 us
    gather x2, local copies, waits for them, and re-layouts, toeplitz(): lower = jnp.take(taps, jnp.clip(offset, 0, LONG_TAPS - 1), axis=0)  62.6 us
    all_gather x1, waiting for transfers between devices, per_device(): lax.all_gather(scaled.astype(jnp.bfloat16), 'tp', axis=1, tiled=True)  48.7 us
    dot_general x3, matrix products, add_one(): return jnp.dot(features, piece, preferred_element_type=jnp.float32)  26.9 us
  transfers between devices with their start and end apart: 6, of which 5 were waited for; matrix products, arithmetic and copies ran while one was open for 21% of the time, Pallas kernels for 0%

commit v1 on v0

--- a/solution.py
+++ b/solution.py
@@ -49,7 +49,10 @@
     full_width = width_local * lax.axis_size("tp")
     gain = lax.dynamic_slice_in_dim(norm_gain, lax.axis_index("tp") * width_local, width_local, 0)
     scaled = local_f * lax.rsqrt(total[:, None] / full_width + 1e-06) * gain[None, :]
-    features = lax.all_gather(scaled.astype(jnp.bfloat16), "tp", axis=1, tiled=True)
+    features = jnp.concatenate(
+        lax.all_to_all(jnp.stack([scaled.astype(jnp.bfloat16)] * lax.axis_size("tp")), "tp", 0, 0),
+        axis=1,
+    )
 
     def add_one(piece):
         return jnp.dot(features, piece, preferred_element_type=jnp.float32)

time: 710 us -> 653 us (0.920)
  waiting for transfers between devices: 486 us -> 419 us
  starting transfers between devices: 3.36 us -> 10.5 us
    all_gather x3, waiting for transfers between devices: 429 us -> 360 us  [project_stream(): return add_one(lax.all_gather(weight, 'ctx', axis=0, tiled=True))]
    all_to_all x0 -> x1, waiting for transfers between devices: none -> 50.1 us  [per_device(): lax.all_to_all(jnp.stack([scaled.astype(jnp.bfloat16)] * lax.axis_size('t...]
    all_gather x1 -> x0, waiting for transfers between devices: 48.7 us -> none  [per_device(): lax.all_gather(scaled.astype(jnp.bfloat16), 'tp', axis=1, tiled=True)]
    all_to_all x0 -> x1, starting transfers between devices: none -> 7.23 us  [per_device(): lax.all_to_all(jnp.stack([scaled.astype(jnp.bfloat16)] * lax.axis_size('t...]
  transfers between devices with their start and end apart: 6 -> 6, of which waited for: 5 -> 5; matrix products, arithmetic and copies ran while one was open for 21% -> 24% of each run, Pallas kernels for 0% -> 0%
where the time goes in v1:
time: 653 us; the launch traced here: 652 us
  waiting for transfers between devices  419 us (64%)
  local copies, waits for them, and re-layouts  148 us (23%)
  matrix products  33.6 us (5%)
  other arithmetic  22 us (3%)
  between operations  13.4 us (2%)
  starting transfers between devices  10.5 us (2%)
    all_gather x3, waiting for transfers between devices, project_stream(): return add_one(lax.all_gather(weight, 'ctx', axis=0, tiled=True))  360 us
    gather x2, local copies, waits for them, and re-layouts, toeplitz(): jnp.take(taps, jnp.clip(offset + LONG_TAPS, 0, LONG_TAPS - 1), axis=0)  63.5 us
    gather x2, local copies, waits for them, and re-layouts, toeplitz(): lower = jnp.take(taps, jnp.clip(offset, 0, LONG_TAPS - 1), axis=0)  62.6 us
    all_to_all x1, waiting for transfers between devices, per_device(): lax.all_to_all(jnp.stack([scaled.astype(jnp.bfloat16)] * lax.axis_size('t...  50.1 us
    dot_general x3, matrix products, add_one(): return jnp.dot(features, piece, preferred_element_type=jnp.float32)  27 us
    add x1, other arithmetic, short_conv(): total = total + filt[:, k, None, :] * window  13.8 us
  transfers between devices with their start and end apart: 6, of which 5 were waited for; matrix products, arithmetic and copies ran while one was open for 24% of the time, Pallas kernels for 0%

profile of v1, /device:TPU:8, one launch (start us, length us, event | category | flops | bytes accessed | tf_op | source)
XLA Modules:
  0.0 652.3 jit_solution(14368022871548475634)
XLA Ops:
  6.5 1.9 fusion.56
  12.1 5.7 psum.7
  18.7 2.3 stack.19
  21.0 7.2 %all-to-all-start = ((bf16[4,512,1024]{1,2,0:T(8,128)(2,1)}), bf16[4,512,1024]{1,2,0:T(8,128)(2,1)}, u32[]{:S(2)}, u32[]{:S(2)}) async-start(bf16[4,512,1024]{1,2,0:T(8,128)(2,1)} %stack.19), calls=%async_computation | async-start | bytes 8388608 | tf_op jit(solution)/shard_map/all_to_all | solution.py:53
  28.7 50.1 %all-to-all-done = bf16[4,512,1024]{1,2,0:T(8,128)(2,1)} async-done(((bf16[4,512,1024]{1,2,0:T(8,128)(2,1)}), bf16[4,512,1024]{1,2,0:T(8,128)(2,1)}, u32[]{:S(2)}, u32[]{:S(2)}) %all-to-all-start) | async-done | bytes 4194336 | tf_op jit(solution)/shard_map/all_to_all | solution.py:53
  78.7 84.0 %all-gather.7.cloned.1.call-done = bf16[1,4096,1024]{2,1,0:T(8,128)(2,1)} async-done(((bf16[1,64,1024]{2,1,0:T(8,128)(2,1)}), bf16[1,4096,1024]{2,1,0:T(8,128)(2,1)}) %all-gather.7.cloned.1.call-update) | async-done | bytes 8388624 | tf_op jit(solution)/shard_map/all_gather | solution.py:61
  162.8 8.2 %fusion.26 = f32[1,512,1024]{2,1,0:T(8,128)S(1)} fusion(bf16[512,4096]{0,1:T(8,128)(2,1)} %bitcast.1, bf16[1,4096,1024]{2,1,0:T(8,128)(2,1)} %all-gather.7.cloned.1.call-done), kind=kOutput, calls=%fused_computation.47 | convolution fusion | flops 4294967296 | bytes 14680064 | tf_op jit(solution)/shard_map/dot_general | solution.py:58
  171.0 139.3 %all-gather.9.cloned.1.call-done = bf16[1,4096,1024]{2,1,0:T(8,128)(2,1)} async-done(((bf16[1,64,1024]{2,1,0:T(8,128)(2,1)}), bf16[1,4096,1024]{2,1,0:T(8,128)(2,1)}) %all-gather.9.cloned.1.call-update) | async-done | bytes 8388624 | tf_op jit(solution)/shard_map/all_gather | solution.py:61
  310.2 10.5 %fusion.29 = f32[1,512,1024]{2,1,0:T(8,128)} fusion(bf16[512,4096]{0,1:T(8,128)(2,1)} %bitcast.1, bf16[1,4096,1024]{2,1,0:T(8,128)(2,1)} %all-gather.9.cloned.1.call-done), kind=kOutput, calls=%fused_computation.48 | convolution fusion | flops 4294967296 | bytes 14680064 | tf_op jit(solution)/shard_map/dot_general | solution.py:58
  320.8 137.0 %all-gather.11.cloned.1.call-done = bf16[1,4096,1024]{2,1,0:T(8,128)(2,1)} async-done(((bf16[1,64,1024]{2,1,0:T(8,128)(2,1)}), bf16[1,4096,1024]{2,1,0:T(8,128)(2,1)}) %all-gather.11.cloned.1.call-update) | async-done | bytes 8388624 | tf_op jit(solution)/shard_map/all_gather | solution.py:61
  457.8 8.3 %fusion.32 = f32[1,512,1024]{2,1,0:T(8,128)S(1)} fusion(bf16[512,4096]{0,1:T(8,128)(2,1)} %bitcast.1, bf16[1,4096,1024]{2,1,0:T(8,128)(2,1)} %all-gather.11.cloned.1.call-done), kind=kOutput, calls=%fused_computation.49 | convolution fusion | flops 4294967296 | bytes 14680064 | tf_op jit(solution)/shard_map/dot_general | solution.py:58
  470.6 57.8 %gather_fusion.1 = bf16[16384,64]{1,0:T(8,128)(2,1)} fusion(bf16[128,64]{1,0:T(8,128)(2,1)S(1)} %multiply_convert_fusion, s32[16384]{0:T(1024)S(1)} %bitcast_clamp_fusion), kind=kCustom, calls=%fused_computation.1.clone | custom fusion | bytes 4259840 | tf_op jit(solution)/shard_map/jit(_take)/gather | solution.py:25
  528.4 5.7 copy.21
  534.1 57.8 %gather_fusion = bf16[16384,64]{1,0:T(8,128)(2,1)} fusion(bf16[128,64]{1,0:T(8,128)(2,1)S(1)} %multiply_convert_fusion, s32[16384]{0:T(1024)S(1)} %bitcast_clamp_fusion.1), kind=kCustom, calls=%fused_computation.clone | custom fusion | bytes 4259840 | tf_op jit(solution)/shard_map/jit(_take)/gather | solution.py:24
  591.9 4.8 copy.18
  596.7 13.8 %multiply_add_fusion = f32[3,512,1024]{2,1,0:T(8,128)S(1)} fusion(bf16[3,512,1024]{2,1,0:T(8,128)(2,1)} %copy-done.3, bf16[3,6,1024]{2,1,0:T(8,128)(2,1)S(1)} %collective-permute-done, f32[3,1024]{1,0:T(4,128)S(1)} %get-tuple-element.18, f32[3,1024]{1,0:T(4,128)S(1)} %get-tuple-element.19, f32[3,1024]{1,0:T(4,128)S(1)} %get-tuple-element.20, ...), kind=kLoop, calls=%fused_computation.15 | loop fusion | flops 59768832 | bytes 9560064 | tf_op jit(solution)/shard_map/add | solution.py:37
  610.5 2.7 copy-done.2
  618.4 2.5 fusion.62
  620.9 6.9 %collective-permute-done.1 = bf16[128,1024]{1,0:T(8,128)(2,1)S(1)} collective-permute-done((bf16[128,1024]{1,0:T(8,128)(2,1)}, bf16[128,1024]{1,0:T(8,128)(2,1)S(1)}, u32[]{:S(2)}, u32[]{:S(2)}) %collective-permute-start.1) | collective-permute-done | bytes 262176 | tf_op jit(solution)/shard_map/ppermute | solution.py:14
  628.9 2.3 copy.20
  631.2 2.1 slice.97
  633.3 3.5 fusion.18
  640.9 2.0 copy.24
  642.9 2.9 fusion.17
  (53 shorter events, 19.6 us)
Async XLA Ops:
  6.5 4.1 copy-start
  6.5 156.2 %all-gather.7.cloned.1.call-start = ((), (), s32[]{:S(2)}) async-start(), calls=%async_computation.1 | async-start | bytes 8519680 | tf_op jit(solution)/shard_map/all_gather | solution.py:61
  8.4 301.8 %all-gather.9.cloned.1.call-start = ((), (), s32[]{:S(2)}) async-start(), calls=%async_computation.2 | async-start | bytes 8519680 | tf_op jit(solution)/shard_map/all_gather | solution.py:61
  9.2 448.6 %all-gather.11.cloned.1.call-start = ((), (), s32[]{:S(2)}) async-start(), calls=%async_computation.3 | async-start | bytes 8519680 | tf_op jit(solution)/shard_map/all_gather | solution.py:61
  21.0 7.2 %copy-start.6 = (f32[128,64]{0,1:T(8,128)S(1)}, f32[128,64]{0,1:T(8,128)}, u32[]{:S(2)}) copy-start(f32[128,64]{0,1:T(8,128)} %param.16) | copy-start | bytes 98308
  21.0 7.3 %copy-start.8 = (f32[64]{0:T(128)S(1)}, f32[64]{0:T(128)}, u32[]{:S(2)}) copy-start(f32[64]{0:T(128)} %param.17) | copy-start | bytes 772
  21.0 7.5 %copy-start.5 = (f32[3,7,1024]{2,1,0:T(8,128)S(1)}, f32[3,7,1024]{2,1,0:T(8,128)}, u32[]{:S(2)}) copy-start(f32[3,7,1024]{2,1,0:T(8,128)} %param.15) | copy-start | bytes 258052
  21.0 57.7 %all-to-all-start = ((bf16[4,512,1024]{1,2,0:T(8,128)(2,1)}), bf16[4,512,1024]{1,2,0:T(8,128)(2,1)}, u32[]{:S(2)}, u32[]{:S(2)}) async-start(bf16[4,512,1024]{1,2,0:T(8,128)(2,1)} %stack.19), calls=%async_computation | async-start | bytes 8388608 | tf_op jit(solution)/shard_map/all_to_all | solution.py:53
  320.7 145.4 %copy-start.7 = (f32[3,1024]{1,0:T(4,128)S(1)}, f32[3,1024]{1,0:T(4,128)}, u32[]{:S(2)}) copy-start(f32[3,1024]{1,0:T(4,128)} %param.14) | copy-start | bytes 36868
  457.8 8.4 %copy-start.4 = (f32[1,512,1024]{2,1,0:T(8,128)S(1)}, f32[1,512,1024]{2,1,0:T(8,128)}, u32[]{:S(2)}) copy-start(f32[1,512,1024]{2,1,0:T(8,128)} %fusion.29) | copy-start | bytes 6291460
  467.1 1.7 copy-start.3
  468.8 127.9 %collective-permute-start = (bf16[3,6,1024]{2,1,0:T(8,128)(2,1)S(1)}, bf16[3,6,1024]{2,1,0:T(8,128)(2,1)S(1)}, u32[]{:S(2)}, u32[]{:S(2)}) collective-permute-start(bf16[3,6,1024]{2,1,0:T(8,128)(2,1)S(1)} %slice.102), channel_id=1, source_target_pairs={{0,4},{4,8},{8,12},{12,16},{16,20},{20,24},{24,28},{28,32},{32,36}... | collective-permute-start | bytes 110600 | tf_op jit(solution)/shard_map/ppermute | solution.py:14
  610.5 2.7 copy-start.2
  615.5 12.3 %collective-permute-start.1 = (bf16[128,1024]{1,0:T(8,128)(2,1)}, bf16[128,1024]{1,0:T(8,128)(2,1)S(1)}, u32[]{:S(2)}, u32[]{:S(2)}) collective-permute-start(bf16[128,1024]{1,0:T(8,128)(2,1)} %slice_bitcast_fusion.1), channel_id=1, source_target_pairs={{0,4},{4,8},{8,12},{12,16},{16,20},{20,24},{24,28},{28,32},{32,36}... | collective-permute-start | bytes 786440 | tf_op jit(solution)/shard_map/ppermute | solution.py:14
  640.9 4.9 copy-start.1
Sparse Core Ops, SparseCore 0:
  10.8 151.8 all-gather.6
  166.2 143.9 all-gather.8
  313.7 143.9 all-gather.10
